TPU v7x, 32 devices: a whole 2x2x4 slice. The times are simulated.
32 devices in a mesh: row: 8 (over y, x, core), col: 4 (over z).
Axes of the slice: x: 2, y: 2, z: 4, core: 2. Of those that a mesh axis runs over, the one named last changes fastest.
Arguments:
- matrix: float32 [9216, 9216], P('row', 'col'), as said below
Outputs:
- factored: float32 [9216, 9216], P('row', 'col')
Inputs may be any that keep to these rules, and one draw needn't show every extreme that they name: `matrix`: Off-diagonal entries are of order one; each diagonal entry lies between 4 * sqrt(256) and 8 * sqrt(256) times that.
All inputs are finite; a program needn't handle non-finite values.
Results may differ from a plain program's by a relative error of at most 0.0001.
Values sent between devices are 32-bit elements; how exact they have to be, the bound alone decides.
No kernel may reach another device: no remote copies, remote signals or barrier semaphores. Data moves between devices by JAX's collectives and lax.ppermute only.
A program may use at most 128 MiB of HBM per device.

v0:
```python
import jax
import jax.numpy as jnp
from jax import lax
from jax.sharding import PartitionSpec as P

B = 256
STEPS = 2


def from_root(array, axis, root):
    mine = lax.axis_index(axis) == root
    return lax.psum(jnp.where(mine, array, jnp.zeros_like(array)), axis)


def mult(left, right):
    return jnp.dot(left, right, precision=lax.Precision.HIGHEST, preferred_element_type=jnp.float32)


def spans(lead, width, extent):
    result = []
    for owner in range(lead // extent, (lead + width - 1) // extent + 1):
        low = max(lead, owner * extent) - owner * extent
        high = min(lead + width, (owner + 1) * extent) - owner * extent
        result.append((owner, low, high))
    return result


def cols_plain(tile, lead, cols):
    pieces = [
        from_root(tile[:, low:high], "col", owner) for owner, low, high in spans(lead, B, cols)
    ]
    return pieces[0]


def rows_joined(stacked, lead, rows):
    pieces = [
        from_root(stacked[low:high], "row", owner) for owner, low, high in spans(lead, B, rows)
    ]
    return jnp.concatenate(pieces, axis=0)


def inverse_of(block, eye):
    inverse = 1.0 / jnp.diagonal(block)
    first = inverse[:, None] * (2.0 * eye - block * inverse[None, :])
    return mult(first, 2.0 * eye - mult(block, first))


def on_device(matrix):
    rows, cols = matrix.shape
    row_ids = lax.axis_index("row") * rows + jnp.arange(rows, dtype=jnp.int32)[:, None]
    col_ids = lax.axis_index("col") * cols + jnp.arange(cols, dtype=jnp.int32)[None, :]
    eye = jnp.eye(B, dtype=jnp.float32)
    tile = matrix
    for step in range(STEPS):
        lead = step * B
        panel = cols_plain(tile, lead, cols)
        joined = rows_joined(jnp.concatenate([tile, panel], axis=1), lead, rows)
        upper = joined[:, :cols]
        lower = mult(panel, inverse_of(joined[:, cols:], eye))
        update = mult(lower, upper)
        picked = jnp.take(lower, jnp.clip(col_ids[0] - lead, 0, B - 1), axis=1)
        below = row_ids >= lead + B
        right = col_ids >= lead + B
        inside = (col_ids >= lead) & (col_ids < lead + B)
        tile = jnp.where(below & right, tile - update, jnp.where(below & inside, picked, tile))
    return tile


def solution(mesh):
    return jax.shard_map(
        on_device,
        mesh=mesh,
        in_specs=(P("row", "col"),),
        out_specs=P("row", "col"),
        check_vma=False,
    )
```

profile of v0, /device:TPU:0, one launch (start us, length us, event | category | flops | bytes accessed | tf_op | source)
XLA Modules:
  0.0 363.7 jit_solution(15044023038616365987)
XLA Ops:
  6.5 0.0 all-reduce.5.cloned.1.call-start
  6.5 2.4 slice_select_fusion.1
  8.9 0.0 all-reduce.5.cloned.1.call-update
  8.9 0.0 all-reduce.7.cloned.1.call-start
  9.0 59.5 %all-reduce.5.cloned.1.call-done = f32[1152,256]{1,0:T(8,128)} async-done(((f32[1152,256]{1,0:T(8,128)}), f32[1152,256]{1,0:T(8,128)}) %all-reduce.5.cloned.1.call-update) | async-done | bytes 1179664 | tf_op jit(solution)/shard_map/psum | solution.py:12
  68.5 3.6 fusion.3
  72.0 0.0 copy-start.1
  72.0 0.0 all-reduce.7.cloned.1.call-update
  72.1 0.0 all-reduce.9.cloned.1.call-start
  72.1 0.6 fusion.37
  72.7 0.6 compare_and_fusion.1
  73.3 0.6 fusion.33
  74.0 62.3 %all-reduce.7.cloned.1.call-done = f32[256,2560]{1,0:T(8,128)} async-done(((f32[256,2560]{1,0:T(8,128)}), f32[256,2560]{1,0:T(8,128)}) %all-reduce.7.cloned.1.call-update) | async-done | bytes 2621456 | tf_op jit(solution)/shard_map/psum | solution.py:12
  136.3 1.0 slice.40
  137.3 2.3 gather_fusion
  139.6 1.5 convolution_subtract_fusion.3
  141.1 1.4 fusion.11
  142.5 0.0 copy-done.1
  142.5 1.1 fusion.51
  143.6 0.4 copy.6
  144.0 8.8 %gather_fusion.2 = f32[2304,1152]{1,0:T(8,128)} fusion(f32[1152,256]{0,1:T(8,128)S(1)} %copy.6, s32[3072]{0:T(1024)S(1)} %pad_clamp_fusion.1), kind=kCustom, calls=%fused_computation.clone | custom fusion | bytes 21242880 | tf_op jit(solution)/shard_map/jit(_take)/gather | solution.py:61
  152.8 0.0 copy-start.3
  152.8 0.0 copy-start.6
  152.8 0.0 copy-start.7
  152.8 0.0 copy-start.9
  152.8 12.7 %copy.7 = f32[2304,1152]{0,1:T(8,128)} copy(f32[2304,1152]{1,0:T(8,128)} %gather_fusion.2) | data formatting | bytes 21233664 | tf_op jit(solution)/shard_map/jit(_take)/gather | solution.py:61
  165.5 0.0 copy-done.3
  165.5 0.0 copy-done.6
  165.5 0.0 copy-done.7
  165.5 0.0 copy-done.9
  165.5 16.1 %fusion.1 = f32[1152,2304]{1,0:T(8,128)S(1)} fusion(f32[1152,2304]{1,0:T(8,128)} %param.3, f32[1152,256]{1,0:T(8,128)S(1)} %fusion.51, f32[2304,1152]{0,1:T(8,128)} %copy.7, pred[2304]{0:T(1024)(128)(4,1)S(1)} %copy-done.3, pred[2304]{0:T(1024)(128)(4,1)S(1)} %copy-done.7, pred[2304]{0:T(1024)(128)(4,1)S(1)} %copy-done.6, pred[1152]{0:T(1024)(128)(4,1)S(1)} %copy-done.9, ...), kind=kOutput, calls=%fused_computation.7 | convolution fusion | flops 8169652224 | bytes 35397504 | tf_op jit(solution)/shard_map/dot_general | solution.py:16
  181.6 0.0 copy-start
  181.6 4.1 %copy-done = f32[1152,2304]{1,0:T(8,128)} copy-done((f32[1152,2304]{1,0:T(8,128)}, f32[1152,2304]{1,0:T(8,128)S(1)}, u32[]{:S(2)}) %copy-start) | copy-done | bytes 10616856
  185.7 1.1 slice_select_fusion
  186.8 0.0 all-reduce.9.cloned.1.call-update
  186.9 0.2 all-reduce.11.cloned.1.call-start
  187.1 55.4 %all-reduce.9.cloned.1.call-done = f32[1152,256]{1,0:T(8,128)} async-done(((f32[1152,256]{1,0:T(8,128)}), f32[1152,256]{1,0:T(8,128)}) %all-reduce.9.cloned.1.call-update) | async-done | bytes 1179664 | tf_op jit(solution)/shard_map/psum | solution.py:12
  242.5 3.6 fusion.2
  246.2 0.0 copy-start.2
  246.2 0.0 all-reduce.11.cloned.1.call-update
  246.2 0.6 fusion.38
  246.8 0.6 fusion.34
  247.4 63.0 %all-reduce.11.cloned.1.call-done = f32[256,2560]{1,0:T(8,128)} async-done(((f32[256,2560]{1,0:T(8,128)}), f32[256,2560]{1,0:T(8,128)}) %all-reduce.11.cloned.1.call-update) | async-done | bytes 2621456 | tf_op jit(solution)/shard_map/psum | solution.py:12
  310.4 1.0 slice.43
  311.4 2.3 gather_fusion.1
  313.7 1.5 convolution_subtract_fusion.2
  315.2 1.4 fusion.8
  316.6 0.0 copy-done.2
  316.6 1.1 fusion.52
  317.7 0.4 copy.8
  318.1 8.9 %gather_fusion.3 = f32[2304,1152]{1,0:T(8,128)} fusion(f32[1152,256]{0,1:T(8,128)S(1)} %copy.8, s32[3072]{0:T(1024)S(1)} %pad_clamp_fusion), kind=kCustom, calls=%fused_computation.1.clone | custom fusion | bytes 21242880 | tf_op jit(solution)/shard_map/jit(_take)/gather | solution.py:61
  327.0 0.0 copy-start.4
  327.0 0.0 copy-start.5
  327.0 0.0 copy-start.8
  327.0 12.7 %copy.9 = f32[2304,1152]{0,1:T(8,128)} copy(f32[2304,1152]{1,0:T(8,128)} %gather_fusion.3) | data formatting | bytes 21233664 | tf_op jit(solution)/shard_map/jit(_take)/gather | solution.py:61
  339.7 0.0 copy-done.4
  339.7 0.0 copy-done.5
  339.7 0.0 copy-done.8
  339.7 17.5 %fusion = f32[1152,2304]{1,0:T(8,128)} fusion(f32[1152,2304]{1,0:T(8,128)} %copy-done, f32[1152,256]{1,0:T(8,128)S(1)} %fusion.52, f32[2304,1152]{0,1:T(8,128)} %copy.9, pred[2304]{0:T(1024)(128)(4,1)S(1)} %compare_and_fusion, pred[2304]{0:T(1024)(128)(4,1)S(1)} %copy-done.5, pred[2304]{0:T(1024)(128)(4,1)S(1)} %copy-done.4, ...), kind=kOutput, calls=%fused_computation.5 | convolution fusion | flops 8169652224 | bytes 35397504 | tf_op jit(solution)/shard_map/dot_general | solution.py:16
  (8 shorter events, 0.1 us)
Async XLA Ops:
  6.5 61.9 %all-reduce.5.cloned.1.call-start = ((), (), s32[]{:S(2)}) async-start(), calls=%async_computation | async-start | bytes 2359296 | tf_op jit(solution)/shard_map/psum | solution.py:12
  8.9 127.4 %all-reduce.7.cloned.1.call-start = ((), (), s32[]{:S(2)}) async-start(), calls=%async_computation.1 | async-start | bytes 5242880 | tf_op jit(solution)/shard_map/psum | solution.py:12
  72.0 70.5 %copy-start.1 = (f32[1152,256]{1,0:T(8,128)S(1)}, f32[1152,256]{1,0:T(8,128)}, u32[]{:S(2)}) copy-start(f32[1152,256]{1,0:T(8,128)} %all-reduce.5.cloned.1.call-done) | copy-start | bytes 3538948
  72.1 170.5 %all-reduce.9.cloned.1.call-start = ((), (), s32[]{:S(2)}) async-start(), calls=%async_computation.2 | async-start | bytes 2359296 | tf_op jit(solution)/shard_map/psum | solution.py:12
  152.8 12.7 %copy-start.3 = (pred[2304]{0:T(1024)(128)(4,1)S(1)}, pred[2304]{0:T(1024)(128)(4,1)}, u32[]{:S(2)}) copy-start(pred[2304]{0:T(1024)(128)(4,1)} %compare_and_fusion.1) | copy-start | bytes 6916
  152.8 12.7 %copy-start.6 = (pred[2304]{0:T(1024)(128)(4,1)S(1)}, pred[2304]{0:T(1024)(128)(4,1)}, u32[]{:S(2)}) copy-start(pred[2304]{0:T(1024)(128)(4,1)} %get-tuple-element.6) | copy-start | bytes 6916
  152.8 12.7 %copy-start.7 = (pred[2304]{0:T(1024)(128)(4,1)S(1)}, pred[2304]{0:T(1024)(128)(4,1)}, u32[]{:S(2)}) copy-start(pred[2304]{0:T(1024)(128)(4,1)} %get-tuple-element.7) | copy-start | bytes 6916
  152.8 12.7 %copy-start.9 = (pred[1152]{0:T(1024)(128)(4,1)S(1)}, pred[1152]{0:T(1024)(128)(4,1)}, u32[]{:S(2)}) copy-start(pred[1152]{0:T(1024)(128)(4,1)} %fusion.37) | copy-start | bytes 3460
  181.6 4.1 %copy-start = (f32[1152,2304]{1,0:T(8,128)}, f32[1152,2304]{1,0:T(8,128)S(1)}, u32[]{:S(2)}) copy-start(f32[1152,2304]{1,0:T(8,128)S(1)} %fusion.1) | copy-start | bytes 31850500
  186.9 123.5 %all-reduce.11.cloned.1.call-start = ((), (), s32[]{:S(2)}) async-start(), calls=%async_computation.3 | async-start | bytes 5242880 | tf_op jit(solution)/shard_map/psum | solution.py:12
  246.2 70.5 %copy-start.2 = (f32[1152,256]{1,0:T(8,128)S(1)}, f32[1152,256]{1,0:T(8,128)}, u32[]{:S(2)}) copy-start(f32[1152,256]{1,0:T(8,128)} %all-reduce.9.cloned.1.call-done) | copy-start | bytes 3538948
  327.0 12.7 %copy-start.4 = (pred[2304]{0:T(1024)(128)(4,1)S(1)}, pred[2304]{0:T(1024)(128)(4,1)}, u32[]{:S(2)}) copy-start(pred[2304]{0:T(1024)(128)(4,1)} %get-tuple-element.8) | copy-start | bytes 6916
  327.0 12.7 %copy-start.5 = (pred[2304]{0:T(1024)(128)(4,1)S(1)}, pred[2304]{0:T(1024)(128)(4,1)}, u32[]{:S(2)}) copy-start(pred[2304]{0:T(1024)(128)(4,1)} %get-tuple-element.9) | copy-start | bytes 6916
  327.0 12.7 %copy-start.8 = (pred[1152]{0:T(1024)(128)(4,1)S(1)}, pred[1152]{0:T(1024)(128)(4,1)}, u32[]{:S(2)}) copy-start(pred[1152]{0:T(1024)(128)(4,1)} %fusion.38) | copy-start | bytes 3460
Sparse Core Ops, SparseCore 0:
  9.7 58.6 all-reduce.4
  72.2 64.0 all-reduce.6
  187.0 55.5 all-reduce.8
  246.3 64.0 all-reduce.10
where the time goes:
time: 365 us; the launch traced here: 364 us
  waiting for transfers between devices  240 us (66%)
  local copies, waits for them, and re-layouts  54.6 us (15%)
  matrix products  41.4 us (11%)
  other arithmetic  13.7 us (4%)
  between operations  13.3 us (4%)
    psum x4, waiting for transfers between devices, from_root(): return lax.psum(jnp.where(mine, array, jnp.zeros_like(array)), axis)  240 us
    gather x4, local copies, waits for them, and re-layouts, on_device(): picked = jnp.take(lower, jnp.clip(col_ids[0] - lead, 0, B - 1), axis=1)  43.1 us
    dot_general x8, matrix products, mult(): jnp.dot(left, right, precision=lax.Precision.HIGHEST, preferred_element_t...  41.4 us
    select_n x4, other arithmetic, from_root(): return lax.psum(jnp.where(mine, array, jnp.zeros_like(array)), axis)  10.7 us
  transfers between devices with their start and end apart: 4, of which 4 were waited for; matrix products, arithmetic and copies ran while one was open for 1% of the time, Pallas kernels for 0%

commit v1 on v0

v1 whole, which is shorter than its diff:
```python
import jax
import jax.numpy as jnp
from jax import lax
from jax.experimental import pallas as pl
from jax.experimental.pallas import tpu as pltpu
from jax.sharding import PartitionSpec as P


B = 256
STEPS = 2
W = STEPS * B


def from_root(array, axis, root):
    mine = lax.axis_index(axis) == root
    return lax.psum(jnp.where(mine, array, jnp.zeros_like(array)), axis)


def mult(left, right):
    return jnp.dot(left, right, precision=lax.Precision.HIGHEST, preferred_element_type=jnp.float32)


def spans(lead, width, extent):
    result = []
    for owner in range(lead // extent, (lead + width - 1) // extent + 1):
        low = max(lead, owner * extent) - owner * extent
        high = min(lead + width, (owner + 1) * extent) - owner * extent
        result.append((owner, low, high))
    return result


def joined_from(array, axis, lead, extent, dim):
    pieces = [
        from_root(lax.slice_in_dim(array, low, high, axis=dim), axis, owner)
        for owner, low, high in spans(lead, B, extent)
    ]
    return jnp.concatenate(pieces, axis=dim)


def inverse_of(block, eye):
    inverse = 1.0 / jnp.diagonal(block)
    first = inverse[:, None] * (2.0 * eye - block * inverse[None, :])
    return mult(first, 2.0 * eye - mult(block, first))


def general(tile):
    rows, cols = tile.shape
    row_ids = lax.axis_index("row") * rows + jnp.arange(rows, dtype=jnp.int32)[:, None]
    col_ids = lax.axis_index("col") * cols + jnp.arange(cols, dtype=jnp.int32)[None, :]
    eye = jnp.eye(B, dtype=jnp.float32)
    for step in range(STEPS):
        lead = step * B
        panel = joined_from(tile, "col", lead, cols, 1)
        joined = joined_from(jnp.concatenate([tile, panel], axis=1), "row", lead, rows, 0)
        upper = joined[:, :cols]
        lower = mult(panel, inverse_of(joined[:, cols:], eye))
        update = mult(lower, upper)
        picked = jnp.take(lower, jnp.clip(col_ids[0] - lead, 0, B - 1), axis=1)
        below = row_ids >= lead + B
        right = col_ids >= lead + B
        inside = (col_ids >= lead) & (col_ids < lead + B)
        tile = jnp.where(below & right, tile - update, jnp.where(below & inside, picked, tile))
    return tile


ANY = pl.BlockSpec(memory_space=pl.ANY)
SM = pl.BlockSpec(memory_space=pltpu.SMEM)
VM = pl.BlockSpec(memory_space=pltpu.VMEM)
F32 = jnp.float32
BF16 = jnp.bfloat16


def split(x):
    hi = x.astype(BF16)
    return hi, (x - hi.astype(F32)).astype(BF16)


def dot(a, b):
    return jnp.dot(a, b, preferred_element_type=F32)


def dot3(a, b):
    (ahi, alo), (bhi, blo) = a, b
    return dot(jnp.concatenate([ahi, ahi, alo], 1), jnp.concatenate([bhi, blo, bhi], 0))


def hdot(a, b):
    return jnp.dot(a, b, precision=lax.Precision.HIGHEST, preferred_element_type=F32)


def among(value, members):
    cond = value == members[0]
    for member in members[1:]:
        cond = cond | (value == member)
    return cond


def onchip(shape, dtype=F32):
    return pltpu.VMEM(shape, dtype)


def choose(ids, sources, shapes, cases):
    def body(ids, *refs):
        outs = refs[len(sources):len(sources) + len(shapes)]
        sem = refs[-1]
        for rs, zs, moves in cases:
            cond = None
            if rs is not None:
                cond = among(ids[0], rs)
            if zs is not None:
                other = among(ids[1], zs)
                cond = other if cond is None else cond & other

            @pl.when(cond)
            def _(moves=moves):
                copies = [
                    pltpu.make_async_copy(refs[s].at[view], outs[o].at[to], sem.at[k])
                    for k, (s, view, o, to) in enumerate(moves)
                ]
                for copy in copies:
                    copy.start()
                for copy in copies:
                    copy.wait()

    most = max(len(moves) for _, _, moves in cases)
    return pl.pallas_call(
        body,
        out_shape=tuple(onchip(s) for s in shapes),
        in_specs=[SM] + [ANY] * len(sources),
        out_specs=(VM,) * len(shapes),
        scratch_shapes=[pltpu.SemaphoreType.DMA((most,))],
        compiler_params=pltpu.CompilerParams(vmem_limit_bytes=1 * 2**20),
    )(ids, *sources)


def factors(ids, dcore, dmate):
    def body(ids, dcore, dmate, w_ref, l_ref, d, sem):
        for odd, ref in ((0, dcore), (1, dmate)):

            @pl.when(ids[0] % 2 == odd)
            def _(ref=ref):
                copy = pltpu.make_async_copy(ref, d, sem)
                copy.start()
                copy.wait()

        blk = lambda i, j: d[i * B:(i + 1) * B, j * B:(j + 1) * B]
        eye = (
            lax.broadcasted_iota(jnp.int32, (B, B), 0)
            == lax.broadcasted_iota(jnp.int32, (B, B), 1)
        )

        def second(block):
            diag = jnp.where(eye, block, 0.0)
            down = 1.0 / jnp.sum(diag, axis=1, keepdims=True)
            across = 1.0 / jnp.sum(diag, axis=0, keepdims=True)
            two = jnp.where(eye, 2.0, 0.0)
            first = down * (two - block * across)
            return hdot(first, two - hdot(block, first))

        s0 = second(blk(0, 0))
        upper = blk(0, 1)
        l10 = hdot(blk(1, 0), s0)
        s1 = second(blk(1, 1) - hdot(l10, upper))
        w_ref[:B, :B] = s0
        w_ref[B:, B:] = s1
        w_ref[:B, B:] = -hdot(s0, hdot(upper, s1))
        w_ref[B:, :B] = jnp.zeros((B, B), F32)
        l_ref[...] = l10

    return pl.pallas_call(
        body,
        out_shape=(onchip((W, W)), onchip((B, B))),
        in_specs=[SM, ANY, ANY],
        out_specs=(VM, VM),
        scratch_shapes=[pltpu.VMEM((W, W), F32), pltpu.SemaphoreType.DMA],
        compiler_params=pltpu.CompilerParams(vmem_limit_bytes=8 * 2**20),
        name="factors",
    )(ids, dcore, dmate)


def upper_split(ids, tile, parts):
    cols = tile.shape[1]
    h = W // 4
    table = {
        1: (1, 0, 1, 1),
        2: (2, 13, 3, 4),
        3: (5, 12, 6, 7),
        4: (12, 5, 7, 6),
        5: (13, 2, 4, 3),
        6: (8, 10, 9, 11),
        7: (10, 8, 11, 9),
    }

    def body(ids, tile, *refs):
        parts, (out, buf, sem) = refs[:14], refs[14:]
        r = ids[0]

        @pl.when(r == 0)
        def _():
            for q in range(4):
                pltpu.make_async_copy(
                    tile.at[q * h:(q + 1) * h], buf.at[q], sem.at[q]
                ).start()

        for row, picks in table.items():

            @pl.when(r == row)
            def _(picks=picks):
                for q, k in enumerate(picks):
                    view = parts[k]
                    if k == 1:
                        at = (0, 0, h, 2 * h)[q]
                        view = view.at[at:at + h]
                    pltpu.make_async_copy(view, buf.at[q], sem.at[q]).start()

        for q in range(4):
            pltpu.make_async_copy(tile.at[:h], buf.at[q], sem.at[q]).wait()
            hi, lo = split(buf[q])
            out[q * h:(q + 1) * h] = hi
            out[W + q * h:W + (q + 1) * h] = lo

    return pl.pallas_call(
        body,
        out_shape=onchip((2 * W, cols), BF16),
        in_specs=[SM, ANY] + [ANY] * 14,
        out_specs=VM,
        scratch_shapes=[pltpu.VMEM((4, h, cols), F32), pltpu.SemaphoreType.DMA((4,))],
        compiler_params=pltpu.CompilerParams(vmem_limit_bytes=10 * 2**20),
        name="upper_split",
    )(ids, tile, *parts)


def update_call(ids, tile, lo, hi, sources, wmat, l10, u2, prev):
    rows, cols = tile.shape
    n = hi - lo
    rb = max(d for d in range(16, 385, 16) if n % d == 0)
    count = n // rb
    arrays = [x for item in sources for x in item]
    fast = pltpu.with_memory_space_constraint(tile, pltpu.VMEM)

    def body(*refs):
        ids, tile, wm, l10, u2 = refs[:5]
        parts = refs[5:5 + len(arrays)]
        rest = refs[5 + len(arrays):]
        if prev is not None:
            rest = rest[1:]
        out, pbuf, obuf, psem, osem = rest
        r, z = ids[0], ids[1]
        for place in range(1, 4):

            @pl.when(z == place)
            def _(place=place):
                at = 0
                copies = []
                for k in range(len(sources)):
                    ref = parts[3 * k + place - 1]
                    size = ref.shape[0]
                    copies.append(
                        pltpu.make_async_copy(ref, pbuf.at[at:at + size], psem.at[k])
                    )
                    at += size
                for copy in copies:
                    copy.start()
                for copy in copies:
                    copy.wait()

        @pl.when(z == 0)
        def _():
            pbuf[...] = tile[lo:hi, :W]

        ws = split(wm[...])
        ts = split(l10[...])

        def put(i):
            at = pl.multiple_of(i * rb, rb)
            return pltpu.make_async_copy(
                obuf.at[pl.ds(at, rb)], out.at[pl.ds(lo + at, rb)], osem.at[i]
            )

        def block(i, carry):
            at = pl.multiple_of(i * rb, rb)
            span = pl.ds(at, rb)
            ids_of = r * rows + lo + at + lax.broadcasted_iota(jnp.int32, (rb, 1), 0)
            ps = split(pbuf[span])
            l0 = dot3([x[:, :B] for x in ps], [x[:B, :B] for x in ws])
            l1 = dot3(ps, [x[:, B:] for x in ws])
            l1s = split(jnp.where(ids_of >= W, l1, 0.0))
            l0s = split(jnp.where(ids_of >= B, l0, 0.0) - dot3(l1s, ts))
            top = jnp.concatenate([l0s[0], l1s[0]], 1)
            low = jnp.concatenate([l0s[1], l1s[1]], 1)
            both = jnp.concatenate([top, top], 1)
            for j in range(cols // B):
                part = slice(j * B, (j + 1) * B)
                acc = dot(low, u2[:W, part]) + dot(both, u2[:, part])
                new = tile[pl.ds(lo + at, rb), part] - acc
                if j < STEPS:
                    lower = l0 if j == 0 else l1
                    new = jnp.where((z == 0) & (ids_of >= (j + 1) * B), lower, new)
                obuf[span, part] = new
            put(i).start()
            return carry

        lax.fori_loop(0, count, block, 0)

        def finish(i, carry):
            put(i).wait()
            return carry

        lax.fori_loop(0, count, finish, 0)

    operands = [ids, fast, wmat, l10, u2] + arrays
    specs = [SM, VM, VM, VM, VM] + [ANY] * len(arrays)
    aliases = {}
    if prev is not None:
        aliases = {len(operands): 0}
        operands.append(prev)
        specs.append(ANY)
    return pl.pallas_call(
        body,
        out_shape=jax.ShapeDtypeStruct(tile.shape, tile.dtype),
        in_specs=specs,
        out_specs=ANY,
        scratch_shapes=[
            pltpu.VMEM((n, W), F32),
            pltpu.VMEM((n, cols), F32),
            pltpu.SemaphoreType.DMA((len(sources),)),
            pltpu.SemaphoreType.DMA((count,)),
        ],
        input_output_aliases=aliases,
        compiler_params=pltpu.CompilerParams(vmem_limit_bytes=26 * 2**20),
    )(*operands)


def ring(tile, across):
    rows, cols = tile.shape
    r = lax.axis_index("row")
    z = lax.axis_index("col")
    ids = jnp.stack([r, z]).astype(jnp.int32)

    def col_move(x, who, source, target):
        pairs = [(q * across + source, q * across + target) for q in who]
        return lax.ppermute(x, ("row", "col"), pairs)

    def row_move(x, pairs):
        return lax.ppermute(x, "row", pairs)

    def pick(*args):
        return choose(ids, *args)

    h = W // 4
    base = pltpu.with_memory_space_constraint(tile, pltpu.HBM)
    full = slice(0, W)
    whole = slice(None)
    qs = lambda i, j=None: slice(i * h, (i + 1 if j is None else j) * h)
    marks = [0, B, W] + [W + -(-(rows - W) * k // (TAIL * 32)) * 32 for k in range(1, TAIL)] + [rows]
    names = ["A1", "A2"] + [f"B{k + 1}" for k in range(TAIL)]
    cuts = dict(zip(names, zip(marks, marks[1:])))
    panels = [(0, (slice(*c), full), k, whole) for k, c in enumerate(cuts.values())]
    n = len(names)
    uppers = [(0, qs(1), n, whole), (0, qs(0), n + 1, qs(0)), (0, qs(2, 4), n + 1, qs(1, 3))]
    others = tuple(range(1, 8))
    *own, q2, q134 = pick(
        [base],
        [(hi - lo, W) for lo, hi in cuts.values()] + [(h, cols), (3 * h, cols)],
        [
            ((0,), (0,), panels + uppers),
            ((0,), (1, 2, 3), uppers),
            (others, (0,), panels),
        ],
    )
    every = tuple(range(8))
    got = {}
    for k, x in zip(cuts, own):
        a = col_move(x, every, 0, 2)
        got[k] = (col_move(a, every, 2, 1), a, col_move(a, every, 2, 3))

    um2 = row_move(q2, [(0, 1)])
    um134 = row_move(q134, [(0, 1)])
    (c1,) = pick(
        [base, um2], [(h, cols)],
        [((0,), None, [(0, qs(0), 0, whole)]), ((1,), None, [(1, whole, 0, whole)])],
    )
    c2, c3 = pick(
        [base, um134], [(h, cols), (h, cols)],
        [
            ((0,), None, [(0, qs(2), 0, whole), (0, qs(3), 1, whole)]),
            ((1,), None, [(1, qs(2), 0, whole), (1, qs(1), 1, whole)]),
        ],
    )
    first, second, third = [(0, 2), (1, 5)], [(2, 6), (5, 7)], [(6, 4), (7, 3)]
    g1 = row_move(c1, first)
    g2 = row_move(c2, first)
    g3 = row_move(c3, first)
    f1 = row_move(g1, second)
    f2 = row_move(g2, second)
    h1 = row_move(f1, third)
    near = [(2, 3), (5, 4)]
    sg1 = row_move(g1, near)
    sg2 = row_move(g2, near)
    sg3 = row_move(g3, near)
    sf1 = row_move(f1, [(6, 7), (7, 6)])
    sf2 = row_move(f2, [(6, 7), (7, 6)])
    sh1 = row_move(h1, [(3, 2), (4, 5)])

    def block_rows(key):
        lo, hi = cuts[key]
        (x,) = pick(
            [base, *got[key]], [(B, W)],
            [((0,), (0,), [(0, (slice(lo, hi), full), 0, whole)])]
            + [((0,), (p,), [(p, whole, 0, whole)]) for p in (1, 2, 3)],
        )
        return x

    d1, d2 = block_rows("A1"), block_rows("A2")
    e1 = row_move(d1, [(0, 2)])
    e2 = row_move(d2, [(0, 4)])
    e3 = row_move(d2, [(0, 2)])
    e4 = row_move(d1, [(0, 4)])
    x1 = row_move(e1, [(2, 6)])
    x2 = row_move(e2, [(4, 6)])
    top, low = slice(0, B), slice(B, W)
    (dcore,) = pick(
        [d1, d2, e1, e2, e3, e4, x1, x2], [(W, W)],
        [
            ((row,), None, [(p, whole, 0, top), (q, whole, 0, low)])
            for row, p, q in ((0, 0, 1), (2, 2, 4), (4, 5, 3), (6, 6, 7))
        ],
    )
    dmate = row_move(dcore, [(i, i + 1) for i in range(0, 8, 2)])

    wmat, l10 = factors(ids, dcore, dmate)
    u2 = upper_split(
        ids, base,
        (um2, um134, g1, g2, g3, sg1, sg2, sg3, f1, f2, sf1, sf2, h1, sh1),
    )
    pieces = [got[k] for k in names]
    late = marks[-2]
    out = update_call(ids, tile, 0, late, pieces[:-1], wmat, l10, u2, None)
    return update_call(ids, tile, late, rows, pieces[-1:], wmat, l10, u2, out)


TAIL = 3


def solution(mesh):
    across = mesh.shape["col"]

    def on_device(tile):
        rows, cols = tile.shape
        fits = rows >= 2 * W and cols >= W and rows % 128 == 0 and cols % B == 0
        if fits and mesh.shape["row"] == 8 and across == 4:
            return ring(tile, across)
        return general(tile)

    return jax.shard_map(
        on_device,
        mesh=mesh,
        in_specs=(P("row", "col"),),
        out_specs=P("row", "col"),
        check_vma=False,
    )
```

time: 365 us -> 167 us (0.46)
  the two profiles are of different devices: /device:TPU:0 before, /device:TPU:30 now
where the time goes in v1:
time: 167 us; the launch traced here: 166 us
  waiting for transfers between devices  88.2 us (53%)
  starting transfers between devices  46.9 us (28%)
  Pallas kernels  30.1 us (18%)
    ppermute x15, waiting for transfers between devices, col_move(): return lax.ppermute(x, ('row', 'col'), pairs)  60.5 us
    ppermute x21, starting transfers between devices, row_move(): return lax.ppermute(x, 'row', pairs)  33.5 us
    ppermute x21, waiting for transfers between devices, row_move(): return lax.ppermute(x, 'row', pairs)  27.7 us
    pallas_call x2, Pallas kernels, update_call(): pl.pallas_call(body, out_shape=jax.ShapeDtypeStruct(tile.shape, tile.dtyp...  19.2 us
    ppermute x15, starting transfers between devices, col_move(): return lax.ppermute(x, ('row', 'col'), pairs)  13.4 us
    pallas_call x1, Pallas kernels, factors(): pl.pallas_call(body, out_shape=(onchip((W, W)), onchip((B, B))), in_specs...  5.03 us
    pallas_call x6, Pallas kernels, choose(): pl.pallas_call(body, out_shape=tuple((onchip(s) for s in shapes)), in_spe...  3.63 us
  transfers between devices with their start and end apart: 36, of which 8 were waited for; matrix products, arithmetic and copies ran while one was open for 0% of the time, Pallas kernels for 15%

profile of v1, /device:TPU:30, one launch (start us, length us, event | category | flops | bytes accessed | tf_op | source)
XLA Modules:
  0.0 166.1 jit_solution(9356612770696714490)
XLA Ops:
  0.0 0.1 pad_add_fusion.ids.refs_0_
  0.1 0.7 shard_map.17
  0.7 0.9 collective-permute-start.14
  1.6 0.7 collective-permute-start.13
  2.4 0.7 collective-permute-start.3
  3.1 0.0 collective-permute-done.13.refs_1_.refs_0_
  3.1 0.6 shard_map.21
  3.7 0.7 collective-permute-start.15
  4.4 0.7 collective-permute-start
  5.1 0.7 collective-permute-start.27
  5.8 0.7 collective-permute-start.4
  6.5 0.0 collective-permute-done.27.refs_6_
  6.5 1.3 collective-permute-start.5
  7.8 0.7 collective-permute-start.1
  8.5 0.0 collective-permute-done.4.refs_1_.refs_8_
  8.6 1.3 collective-permute-start.2
  9.9 43.1 %collective-permute-done.5.refs_3_.refs_10_ = f32[256,512]{1,0:T(8,128)S(1)} collective-permute-done((f32[256,512]{1,0:T(8,128)S(1)}, f32[256,512]{1,0:T(8,128)S(1)}, u32[]{:S(2)}, u32[]{:S(2)}) %collective-permute-start.5) | collective-permute-done | bytes 524320 | tf_op jit(solution)/shard_map/ppermute | solution.py:342
  53.0 0.7 collective-permute-start.30
  53.7 0.0 collective-permute-done.1.refs_1_.refs_5_
  53.7 0.7 collective-permute-start.33
  54.4 0.6 shard_map.19.refs_1_
  55.0 0.0 collective-permute-done.15.refs_2_
  55.0 0.7 collective-permute-start.7
  55.7 1.3 collective-permute-start.21
  57.0 0.6 shard_map.22
  57.6 4.9 %collective-permute-done.2.refs_3_.refs_7_ = f32[256,512]{1,0:T(8,128)S(1)} collective-permute-done((f32[256,512]{1,0:T(8,128)S(1)}, f32[256,512]{1,0:T(8,128)S(1)}, u32[]{:S(2)}, u32[]{:S(2)}) %collective-permute-start.2) | collective-permute-done | bytes 524320 | tf_op jit(solution)/shard_map/ppermute | solution.py:342
  62.5 0.7 collective-permute-start.16
  63.2 0.6 shard_map.18.refs_0_
  63.8 0.0 collective-permute-done.30.refs_12_
  63.9 0.7 collective-permute-start.6
  64.6 0.0 collective-permute-done.33.refs_15_
  64.6 0.7 collective-permute-start.8
  65.3 0.7 collective-permute-start.9
  66.0 1.3 collective-permute-start.11
  67.3 1.3 collective-permute-start.10
  68.6 0.7 collective-permute-start.31
  69.3 4.5 %collective-permute-done.21.refs_8_ = f32[128,2304]{1,0:T(8,128)S(1)} collective-permute-done((f32[128,2304]{1,0:T(8,128)S(1)}, f32[128,2304]{1,0:T(8,128)S(1)}, u32[]{:S(2)}, u32[]{:S(2)}) %collective-permute-start.21) | collective-permute-done | bytes 1179680 | tf_op jit(solution)/shard_map/ppermute | solution.py:345
  73.8 13.3 %collective-permute-start.25 = (f32[128,2304]{1,0:T(8,128)S(1)}, f32[128,2304]{1,0:T(8,128)S(1)}, u32[]{:S(2)}, u32[]{:S(2)}) collective-permute-start(f32[128,2304]{1,0:T(8,128)S(1)} %collective-permute-done.21.refs_8_), channel_id=1, source_target_pairs={{24,16},{28,12},{25,17},{29,13},{26,18},{30,14},{27,19},{31,15}} | collective-permute-start | bytes 3538952 | tf_op jit(solution)/shard_map/ppermute | solution.py:345
  87.1 0.7 collective-permute-start.18
  87.8 12.9 %collective-permute-done.10.refs_6_ = f32[256,512]{1,0:T(8,128)S(1)} collective-permute-done((f32[256,512]{1,0:T(8,128)S(1)}, f32[256,512]{1,0:T(8,128)S(1)}, u32[]{:S(2)}, u32[]{:S(2)}) %collective-permute-start.10) | collective-permute-done | bytes 524320 | tf_op jit(solution)/shard_map/ppermute | solution.py:345
  100.8 0.7 collective-permute-start.17
  101.5 1.3 collective-permute-start.22
  102.8 0.7 shard_map.20.dcore
  103.5 1.4 collective-permute-start.12
  104.9 2.2 %collective-permute-done.12.dmate = f32[512,512]{1,0:T(8,128)S(1)} collective-permute-done((f32[512,512]{1,0:T(8,128)S(1)}, f32[512,512]{1,0:T(8,128)S(1)}, u32[]{:S(2)}, u32[]{:S(2)}) %collective-permute-start.12) | collective-permute-done | bytes 1048608 | tf_op jit(solution)/shard_map/ppermute | solution.py:345
  107.1 2.3 %collective-permute-start.23 = (f32[128,2304]{1,0:T(8,128)S(1)}, f32[128,2304]{1,0:T(8,128)S(1)}, u32[]{:S(2)}, u32[]{:S(2)}) collective-permute-start(f32[128,2304]{1,0:T(8,128)S(1)} %collective-permute-done.21.refs_8_), channel_id=1, source_target_pairs={{24,28},{28,24},{25,29},{29,25},{26,30},{30,26},{27,31},{31,27}} | collective-permute-start | bytes 3538952 | tf_op jit(solution)/shard_map/ppermute | solution.py:345
  109.4 0.7 collective-permute-start.26
  110.1 0.7 collective-permute-start.19
  110.9 0.7 collective-permute-start.20
  111.6 8.0 %collective-permute-done.22.refs_9_ = f32[128,2304]{1,0:T(8,128)S(1)} collective-permute-done((f32[128,2304]{1,0:T(8,128)S(1)}, f32[128,2304]{1,0:T(8,128)S(1)}, u32[]{:S(2)}, u32[]{:S(2)}) %collective-permute-start.22) | collective-permute-done | bytes 1179680 | tf_op jit(solution)/shard_map/ppermute | solution.py:345
  119.6 1.9 %collective-permute-start.24 = (f32[128,2304]{1,0:T(8,128)S(1)}, f32[128,2304]{1,0:T(8,128)S(1)}, u32[]{:S(2)}, u32[]{:S(2)}) collective-permute-start(f32[128,2304]{1,0:T(8,128)S(1)} %collective-permute-done.22.refs_9_), channel_id=1, source_target_pairs={{24,28},{28,24},{25,29},{29,25},{26,30},{30,26},{27,31},{31,27}} | collective-permute-start | bytes 3538952 | tf_op jit(solution)/shard_map/ppermute | solution.py:345
  121.5 1.3 collective-permute-start.32
  122.8 0.7 collective-permute-start.34
  123.6 1.3 collective-permute-start.35
  124.9 0.7 collective-permute-start.28
  125.6 1.3 collective-permute-start.29
  126.9 0.0 slice-start
  126.9 5.0 %factors.1 = (f32[512,512]{1,0:T(8,128)S(1)}, f32[256,256]{1,0:T(8,128)S(1)}) custom-call(s32[2]{0:T(128)S(1)} %pad_add_fusion.ids.refs_0_, f32[512,512]{1,0:T(8,128)S(1)} %shard_map.20.dcore, f32[512,512]{1,0:T(8,128)S(1)} %collective-permute-done.12.dmate), custom_call_target="tpu_custom_call" | custom-call | tf_op jit(solution)/shard_map/factors/pallas_call | solution.py:170
  131.9 0.0 slice-start.1
  131.9 2.3 %upper_split.1.refs_4_ = bf16[1024,2304]{1,0:T(8,128)(2,1)S(1)} custom-call(s32[2]{0:T(128)S(1)} %pad_add_fusion.ids.refs_0_, f32[1152,2304]{1,0:T(8,128)} %refs_1_.3, f32[128,2304]{1,0:T(8,128)S(1)} %collective-permute-done.13.refs_1_.refs_0_, f32[384,2304]{1,0:T(8,128)S(1)} %collective-permute-done.14.refs_1_, ...), custom_call_target="tpu_custom_call" | custom-call | tf_op jit(solution)/shard_map/upper_split/pallas_call | solution.py:222
  134.2 2.6 %collective-permute-done.32.refs_13_ = f32[224,512]{1,0:T(8,128)S(1)} collective-permute-done((f32[224,512]{1,0:T(8,128)S(1)}, f32[224,512]{1,0:T(8,128)S(1)}, u32[]{:S(2)}, u32[]{:S(2)}) %collective-permute-start.32) | collective-permute-done | bytes 458784 | tf_op jit(solution)/shard_map/ppermute | solution.py:342
  136.8 9.8 %collective-permute-done.35.refs_16_ = f32[224,512]{1,0:T(8,128)S(1)} collective-permute-done((f32[224,512]{1,0:T(8,128)S(1)}, f32[224,512]{1,0:T(8,128)S(1)}, u32[]{:S(2)}, u32[]{:S(2)}) %collective-permute-start.35) | collective-permute-done | bytes 458784 | tf_op jit(solution)/shard_map/ppermute | solution.py:342
  146.7 14.7 %shard_map.23.refs_8_ = f32[1152,2304]{1,0:T(8,128)} custom-call(s32[2]{0:T(128)S(1)} %pad_add_fusion.ids.refs_0_, f32[1152,2304]{1,0:T(8,128)S(1)} %bitcast.3, f32[512,512]{1,0:T(8,128)S(1)} %get-tuple-element.18.refs_2_, f32[256,256]{1,0:T(8,128)S(1)} %get-tuple-element.19.refs_3_, bf16[1024,2304]{1,0:T(8,128)(2,1)S(1)} %upper_split.1.refs_4_, ...), custom_call_target="tpu_custom_call" | custom-call | tf_op jit(solution)/shard_map/pallas_call | solution.py:318
  161.4 4.5 %shard_map.24 = f32[1152,2304]{1,0:T(8,128)} custom-call(s32[2]{0:T(128)S(1)} %pad_add_fusion.ids.refs_0_, f32[1152,2304]{1,0:T(8,128)S(1)} %bitcast.3, f32[512,512]{1,0:T(8,128)S(1)} %get-tuple-element.18.refs_2_, f32[256,256]{1,0:T(8,128)S(1)} %get-tuple-element.19.refs_3_, ...), custom_call_target="tpu_custom_call", output_to_operand_aliasing={{}: (8, {})} | custom-call | tf_op jit(solution)/shard_map/pallas_call | solution.py:318
  (26 shorter events, 0.1 us)
Async XLA Ops:
  0.7 54.9 %collective-permute-start.14 = (f32[384,2304]{1,0:T(8,128)S(1)}, f32[384,2304]{1,0:T(8,128)S(1)}, u32[]{:S(2)}, u32[]{:S(2)}) collective-permute-start(f32[384,2304]{1,0:T(8,128)S(1)} %get-tuple-element.21), channel_id=1, source_target_pairs={{0,4},{1,5},{2,6},{3,7}} | collective-permute-start | bytes 10616840 | tf_op jit(solution)/shard_map/ppermute | solution.py:345
  1.6 1.4 collective-permute-start.13
  2.4 3.4 %collective-permute-start.3 = (f32[256,512]{1,0:T(8,128)S(1)}, f32[256,512]{1,0:T(8,128)S(1)}, u32[]{:S(2)}, u32[]{:S(2)}) collective-permute-start(f32[256,512]{1,0:T(8,128)S(1)} %get-tuple-element.17), channel_id=1, source_target_pairs={{0,2},{4,6},{8,10},{12,14},{16,18},{20,22},{24,26},{28,30}} | collective-permute-start | bytes 1572872 | tf_op jit(solution)/shard_map/ppermute | solution.py:342
  3.7 51.3 %collective-permute-start.15 = (f32[128,2304]{1,0:T(8,128)S(1)}, f32[128,2304]{1,0:T(8,128)S(1)}, u32[]{:S(2)}, u32[]{:S(2)}) collective-permute-start(f32[128,2304]{1,0:T(8,128)S(1)} %shard_map.21), channel_id=1, source_target_pairs={{0,8},{4,20},{1,9},{5,21},{2,10},{6,22},{3,11},{7,23}} | collective-permute-start | bytes 3538952 | tf_op jit(solution)/shard_map/ppermute | solution.py:345
  4.4 3.4 %collective-permute-start = (f32[256,512]{1,0:T(8,128)S(1)}, f32[256,512]{1,0:T(8,128)S(1)}, u32[]{:S(2)}, u32[]{:S(2)}) collective-permute-start(f32[256,512]{1,0:T(8,128)S(1)} %get-tuple-element.16), channel_id=1, source_target_pairs={{0,2},{4,6},{8,10},{12,14},{16,18},{20,22},{24,26},{28,30}} | collective-permute-start | bytes 1572872 | tf_op jit(solution)/shard_map/ppermute | solution.py:342
  5.1 1.4 collective-permute-start.27
  5.8 2.7 %collective-permute-start.4 = (f32[256,512]{1,0:T(8,128)S(1)}, f32[256,512]{1,0:T(8,128)S(1)}, u32[]{:S(2)}, u32[]{:S(2)}) collective-permute-start(f32[256,512]{1,0:T(8,128)S(1)} %collective-permute-done.3.refs_2_.refs_9_), channel_id=1, source_target_pairs={{2,1},{6,5},{10,9},{14,13},{18,17},{22,21},{26,25},{30,29}} | collective-permute-start | bytes 1572872 | tf_op jit(solution)/shard_map/ppermute | solution.py:342
  6.5 46.5 %collective-permute-start.5 = (f32[256,512]{1,0:T(8,128)S(1)}, f32[256,512]{1,0:T(8,128)S(1)}, u32[]{:S(2)}, u32[]{:S(2)}) collective-permute-start(f32[256,512]{1,0:T(8,128)S(1)} %collective-permute-done.3.refs_2_.refs_9_), channel_id=1, source_target_pairs={{2,3},{6,7},{10,11},{14,15},{18,19},{22,23},{26,27},{30,31}} | collective-permute-start | bytes 1572872 | tf_op jit(solution)/shard_map/ppermute | solution.py:342
  7.8 45.8 %collective-permute-start.1 = (f32[256,512]{1,0:T(8,128)S(1)}, f32[256,512]{1,0:T(8,128)S(1)}, u32[]{:S(2)}, u32[]{:S(2)}) collective-permute-start(f32[256,512]{1,0:T(8,128)S(1)} %collective-permute-done.refs_2_.refs_6_), channel_id=1, source_target_pairs={{2,1},{6,5},{10,9},{14,13},{18,17},{22,21},{26,25},{30,29}} | collective-permute-start | bytes 1572872 | tf_op jit(solution)/shard_map/ppermute | solution.py:342
  8.6 54.0 %collective-permute-start.2 = (f32[256,512]{1,0:T(8,128)S(1)}, f32[256,512]{1,0:T(8,128)S(1)}, u32[]{:S(2)}, u32[]{:S(2)}) collective-permute-start(f32[256,512]{1,0:T(8,128)S(1)} %collective-permute-done.refs_2_.refs_6_), channel_id=1, source_target_pairs={{2,3},{6,7},{10,11},{14,15},{18,19},{22,23},{26,27},{30,31}} | collective-permute-start | bytes 1572872 | tf_op jit(solution)/shard_map/ppermute | solution.py:342
  53.0 10.9 %collective-permute-start.30 = (f32[224,512]{1,0:T(8,128)S(1)}, f32[224,512]{1,0:T(8,128)S(1)}, u32[]{:S(2)}, u32[]{:S(2)}) collective-permute-start(f32[224,512]{1,0:T(8,128)S(1)} %get-tuple-element.25), channel_id=1, source_target_pairs={{0,2},{4,6},{8,10},{12,14},{16,18},{20,22},{24,26},{28,30}} | collective-permute-start | bytes 1376264 | tf_op jit(solution)/shard_map/ppermute | solution.py:342
  53.7 10.9 %collective-permute-start.33 = (f32[224,512]{1,0:T(8,128)S(1)}, f32[224,512]{1,0:T(8,128)S(1)}, u32[]{:S(2)}, u32[]{:S(2)}) collective-permute-start(f32[224,512]{1,0:T(8,128)S(1)} %get-tuple-element.26), channel_id=1, source_target_pairs={{0,2},{4,6},{8,10},{12,14},{16,18},{20,22},{24,26},{28,30}} | collective-permute-start | bytes 1376264 | tf_op jit(solution)/shard_map/ppermute | solution.py:342
  55.0 10.3 %collective-permute-start.7 = (f32[256,512]{1,0:T(8,128)S(1)}, f32[256,512]{1,0:T(8,128)S(1)}, u32[]{:S(2)}, u32[]{:S(2)}) collective-permute-start(f32[256,512]{1,0:T(8,128)S(1)} %shard_map.19.refs_1_), channel_id=1, source_target_pairs={{0,16},{1,17},{2,18},{3,19}} | collective-permute-start | bytes 1572872 | tf_op jit(solution)/shard_map/ppermute | solution.py:345
  55.7 18.1 %collective-permute-start.21 = (f32[128,2304]{1,0:T(8,128)S(1)}, f32[128,2304]{1,0:T(8,128)S(1)}, u32[]{:S(2)}, u32[]{:S(2)}) collective-permute-start(f32[128,2304]{1,0:T(8,128)S(1)} %collective-permute-done.15.refs_2_), channel_id=1, source_target_pairs={{8,24},{20,28},{9,25},{21,29},{10,26},{22,30},{11,27},{23,31}} | collective-permute-start | bytes 3538952 | tf_op jit(solution)/shard_map/ppermute | solution.py:345
  62.5 39.0 %collective-permute-start.16 = (f32[128,2304]{1,0:T(8,128)S(1)}, f32[128,2304]{1,0:T(8,128)S(1)}, u32[]{:S(2)}, u32[]{:S(2)}) collective-permute-start(f32[128,2304]{1,0:T(8,128)S(1)} %get-tuple-element.22), channel_id=1, source_target_pairs={{0,8},{4,20},{1,9},{5,21},{2,10},{6,22},{3,11},{7,23}} | collective-permute-start | bytes 3538952 | tf_op jit(solution)/shard_map/ppermute | solution.py:345
  63.9 2.1 %collective-permute-start.6 = (f32[256,512]{1,0:T(8,128)S(1)}, f32[256,512]{1,0:T(8,128)S(1)}, u32[]{:S(2)}, u32[]{:S(2)}) collective-permute-start(f32[256,512]{1,0:T(8,128)S(1)} %shard_map.18.refs_0_), channel_id=1, source_target_pairs={{0,8},{1,9},{2,10},{3,11}} | collective-permute-start | bytes 1572872 | tf_op jit(solution)/shard_map/ppermute | solution.py:345
  64.6 2.7 %collective-permute-start.8 = (f32[256,512]{1,0:T(8,128)S(1)}, f32[256,512]{1,0:T(8,128)S(1)}, u32[]{:S(2)}, u32[]{:S(2)}) collective-permute-start(f32[256,512]{1,0:T(8,128)S(1)} %shard_map.19.refs_1_), channel_id=1, source_target_pairs={{0,8},{1,9},{2,10},{3,11}} | collective-permute-start | bytes 1572872 | tf_op jit(solution)/shard_map/ppermute | solution.py:345
  65.3 3.3 %collective-permute-start.9 = (f32[256,512]{1,0:T(8,128)S(1)}, f32[256,512]{1,0:T(8,128)S(1)}, u32[]{:S(2)}, u32[]{:S(2)}) collective-permute-start(f32[256,512]{1,0:T(8,128)S(1)} %shard_map.18.refs_0_), channel_id=1, source_target_pairs={{0,16},{1,17},{2,18},{3,19}} | collective-permute-start | bytes 1572872 | tf_op jit(solution)/shard_map/ppermute | solution.py:345
  66.0 21.1 %collective-permute-start.11 = (f32[256,512]{1,0:T(8,128)S(1)}, f32[256,512]{1,0:T(8,128)S(1)}, u32[]{:S(2)}, u32[]{:S(2)}) collective-permute-start(f32[256,512]{1,0:T(8,128)S(1)} %collective-permute-done.7.refs_3_), channel_id=1, source_target_pairs={{16,24},{17,25},{18,26},{19,27}} | collective-permute-start | bytes 1572872 | tf_op jit(solution)/shard_map/ppermute | solution.py:345
  67.3 33.5 %collective-permute-start.10 = (f32[256,512]{1,0:T(8,128)S(1)}, f32[256,512]{1,0:T(8,128)S(1)}, u32[]{:S(2)}, u32[]{:S(2)}) collective-permute-start(f32[256,512]{1,0:T(8,128)S(1)} %collective-permute-done.6.refs_2_), channel_id=1, source_target_pairs={{8,24},{9,25},{10,26},{11,27}} | collective-permute-start | bytes 1572872 | tf_op jit(solution)/shard_map/ppermute | solution.py:345
  68.6 34.9 %collective-permute-start.31 = (f32[224,512]{1,0:T(8,128)S(1)}, f32[224,512]{1,0:T(8,128)S(1)}, u32[]{:S(2)}, u32[]{:S(2)}) collective-permute-start(f32[224,512]{1,0:T(8,128)S(1)} %collective-permute-done.30.refs_12_), channel_id=1, source_target_pairs={{2,1},{6,5},{10,9},{14,13},{18,17},{22,21},{26,25},{30,29}} | collective-permute-start | bytes 1376264 | tf_op jit(solution)/shard_map/ppermute | solution.py:342
  73.8 35.5 %collective-permute-start.25 = (f32[128,2304]{1,0:T(8,128)S(1)}, f32[128,2304]{1,0:T(8,128)S(1)}, u32[]{:S(2)}, u32[]{:S(2)}) collective-permute-start(f32[128,2304]{1,0:T(8,128)S(1)} %collective-permute-done.21.refs_8_), channel_id=1, source_target_pairs={{24,16},{28,12},{25,17},{29,13},{26,18},{30,14},{27,19},{31,15}} | collective-permute-start | bytes 3538952 | tf_op jit(solution)/shard_map/ppermute | solution.py:345
  87.1 23.0 %collective-permute-start.18 = (f32[128,2304]{1,0:T(8,128)S(1)}, f32[128,2304]{1,0:T(8,128)S(1)}, u32[]{:S(2)}, u32[]{:S(2)}) collective-permute-start(f32[128,2304]{1,0:T(8,128)S(1)} %collective-permute-done.15.refs_2_), channel_id=1, source_target_pairs={{8,12},{20,16},{9,13},{21,17},{10,14},{22,18},{11,15},{23,19}} | collective-permute-start | bytes 3538952 | tf_op jit(solution)/shard_map/ppermute | solution.py:345
  100.8 10.1 %collective-permute-start.17 = (f32[128,2304]{1,0:T(8,128)S(1)}, f32[128,2304]{1,0:T(8,128)S(1)}, u32[]{:S(2)}, u32[]{:S(2)}) collective-permute-start(f32[128,2304]{1,0:T(8,128)S(1)} %get-tuple-element.23), channel_id=1, source_target_pairs={{0,8},{4,20},{1,9},{5,21},{2,10},{6,22},{3,11},{7,23}} | collective-permute-start | bytes 3538952 | tf_op jit(solution)/shard_map/ppermute | solution.py:345
  101.5 18.1 %collective-permute-start.22 = (f32[128,2304]{1,0:T(8,128)S(1)}, f32[128,2304]{1,0:T(8,128)S(1)}, u32[]{:S(2)}, u32[]{:S(2)}) collective-permute-start(f32[128,2304]{1,0:T(8,128)S(1)} %collective-permute-done.16.refs_3_), channel_id=1, source_target_pairs={{8,24},{20,28},{9,25},{21,29},{10,26},{22,30},{11,27},{23,31}} | collective-permute-start | bytes 3538952 | tf_op jit(solution)/shard_map/ppermute | solution.py:345
  103.5 3.6 %collective-permute-start.12 = (f32[512,512]{1,0:T(8,128)S(1)}, f32[512,512]{1,0:T(8,128)S(1)}, u32[]{:S(2)}, u32[]{:S(2)}) collective-permute-start(f32[512,512]{1,0:T(8,128)S(1)} %shard_map.20.dcore), channel_id=1, source_target_pairs={{0,4},{8,12},{16,20},{24,28},{1,5},{9,13},{17,21},{25,29},{2,6},{1... | collective-permute-start | bytes 3145736 | tf_op jit(solution)/shard_map/ppermute | solution.py:345
  107.1 14.5 %collective-permute-start.23 = (f32[128,2304]{1,0:T(8,128)S(1)}, f32[128,2304]{1,0:T(8,128)S(1)}, u32[]{:S(2)}, u32[]{:S(2)}) collective-permute-start(f32[128,2304]{1,0:T(8,128)S(1)} %collective-permute-done.21.refs_8_), channel_id=1, source_target_pairs={{24,28},{28,24},{25,29},{29,25},{26,30},{30,26},{27,31},{31,27}} | collective-permute-start | bytes 3538952 | tf_op jit(solution)/shard_map/ppermute | solution.py:345
  109.4 13.5 %collective-permute-start.26 = (f32[128,2304]{1,0:T(8,128)S(1)}, f32[128,2304]{1,0:T(8,128)S(1)}, u32[]{:S(2)}, u32[]{:S(2)}) collective-permute-start(f32[128,2304]{1,0:T(8,128)S(1)} %collective-permute-done.25.refs_12_), channel_id=1, source_target_pairs={{12,8},{16,20},{13,9},{17,21},{14,10},{18,22},{15,11},{19,23}} | collective-permute-start | bytes 3538952 | tf_op jit(solution)/shard_map/ppermute | solution.py:345
  110.1 13.4 %collective-permute-start.19 = (f32[128,2304]{1,0:T(8,128)S(1)}, f32[128,2304]{1,0:T(8,128)S(1)}, u32[]{:S(2)}, u32[]{:S(2)}) collective-permute-start(f32[128,2304]{1,0:T(8,128)S(1)} %collective-permute-done.16.refs_3_), channel_id=1, source_target_pairs={{8,12},{20,16},{9,13},{21,17},{10,14},{22,18},{11,15},{23,19}} | collective-permute-start | bytes 3538952 | tf_op jit(solution)/shard_map/ppermute | solution.py:345
  110.9 14.0 %collective-permute-start.20 = (f32[128,2304]{1,0:T(8,128)S(1)}, f32[128,2304]{1,0:T(8,128)S(1)}, u32[]{:S(2)}, u32[]{:S(2)}) collective-permute-start(f32[128,2304]{1,0:T(8,128)S(1)} %collective-permute-done.17.refs_4_), channel_id=1, source_target_pairs={{8,12},{20,16},{9,13},{21,17},{10,14},{22,18},{11,15},{23,19}} | collective-permute-start | bytes 3538952 | tf_op jit(solution)/shard_map/ppermute | solution.py:345
  119.6 6.0 %collective-permute-start.24 = (f32[128,2304]{1,0:T(8,128)S(1)}, f32[128,2304]{1,0:T(8,128)S(1)}, u32[]{:S(2)}, u32[]{:S(2)}) collective-permute-start(f32[128,2304]{1,0:T(8,128)S(1)} %collective-permute-done.22.refs_9_), channel_id=1, source_target_pairs={{24,28},{28,24},{25,29},{29,25},{26,30},{30,26},{27,31},{31,27}} | collective-permute-start | bytes 3538952 | tf_op jit(solution)/shard_map/ppermute | solution.py:345
  121.5 15.3 %collective-permute-start.32 = (f32[224,512]{1,0:T(8,128)S(1)}, f32[224,512]{1,0:T(8,128)S(1)}, u32[]{:S(2)}, u32[]{:S(2)}) collective-permute-start(f32[224,512]{1,0:T(8,128)S(1)} %collective-permute-done.30.refs_12_), channel_id=1, source_target_pairs={{2,3},{6,7},{10,11},{14,15},{18,19},{22,23},{26,27},{30,31}} | collective-permute-start | bytes 1376264 | tf_op jit(solution)/shard_map/ppermute | solution.py:342
  122.8 14.0 %collective-permute-start.34 = (f32[224,512]{1,0:T(8,128)S(1)}, f32[224,512]{1,0:T(8,128)S(1)}, u32[]{:S(2)}, u32[]{:S(2)}) collective-permute-start(f32[224,512]{1,0:T(8,128)S(1)} %collective-permute-done.33.refs_15_), channel_id=1, source_target_pairs={{2,1},{6,5},{10,9},{14,13},{18,17},{22,21},{26,25},{30,29}} | collective-permute-start | bytes 1376264 | tf_op jit(solution)/shard_map/ppermute | solution.py:342
  123.6 23.1 %collective-permute-start.35 = (f32[224,512]{1,0:T(8,128)S(1)}, f32[224,512]{1,0:T(8,128)S(1)}, u32[]{:S(2)}, u32[]{:S(2)}) collective-permute-start(f32[224,512]{1,0:T(8,128)S(1)} %collective-permute-done.33.refs_15_), channel_id=1, source_target_pairs={{2,3},{6,7},{10,11},{14,15},{18,19},{22,23},{26,27},{30,31}} | collective-permute-start | bytes 1376264 | tf_op jit(solution)/shard_map/ppermute | solution.py:342
  124.9 36.5 %collective-permute-start.28 = (f32[192,512]{1,0:T(8,128)S(1)}, f32[192,512]{1,0:T(8,128)S(1)}, u32[]{:S(2)}, u32[]{:S(2)}) collective-permute-start(f32[192,512]{1,0:T(8,128)S(1)} %collective-permute-done.27.refs_6_), channel_id=1, source_target_pairs={{2,1},{6,5},{10,9},{14,13},{18,17},{22,21},{26,25},{30,29}} | collective-permute-start | bytes 1179656 | tf_op jit(solution)/shard_map/ppermute | solution.py:342
  125.6 35.8 %collective-permute-start.29 = (f32[192,512]{1,0:T(8,128)S(1)}, f32[192,512]{1,0:T(8,128)S(1)}, u32[]{:S(2)}, u32[]{:S(2)}) collective-permute-start(f32[192,512]{1,0:T(8,128)S(1)} %collective-permute-done.27.refs_6_), channel_id=1, source_target_pairs={{2,3},{6,7},{10,11},{14,15},{18,19},{22,23},{26,27},{30,31}} | collective-permute-start | bytes 1179656 | tf_op jit(solution)/shard_map/ppermute | solution.py:342
  126.9 19.8 %slice-start = ((s8[10616832]{0:T(1024)(128)(4,1)}), s8[4194304]{0:T(1024)(128)(4,1)S(1)}, s32[]{:S(2)}) async-start(s8[10616832]{0:T(1024)(128)(4,1)} %bitcast.2), calls=%async_computation | async-start | bytes 8388608
  131.9 14.7 %slice-start.1 = ((s8[10616832]{0:T(1024)(128)(4,1)}), s8[4194304]{0:T(1024)(128)(4,1)S(1)}, s32[]{:S(2)}) async-start(s8[10616832]{0:T(1024)(128)(4,1)} %bitcast.2), calls=%async_computation.1 | async-start | bytes 8388608
  131.9 14.7 %slice-start.2 = ((s8[10616832]{0:T(1024)(128)(4,1)}), s8[2228224]{0:T(1024)(128)(4,1)S(1)}, s32[]{:S(2)}) async-start(s8[10616832]{0:T(1024)(128)(4,1)} %bitcast.2), calls=%async_computation.2 | async-start | bytes 4456448

commit v2 on v1

--- a/solution.py
+++ b/solution.py
@@ -84,10 +84,6 @@
     return dot(jnp.concatenate([ahi, ahi, alo], 1), jnp.concatenate([bhi, blo, bhi], 0))
 
 
-def hdot(a, b):
-    return jnp.dot(a, b, precision=lax.Precision.HIGHEST, preferred_element_type=F32)
-
-
 def among(value, members):
     cond = value == members[0]
     for member in members[1:]:
@@ -149,21 +145,24 @@
             == lax.broadcasted_iota(jnp.int32, (B, B), 1)
         )
 
+        def product(a, b):
+            return dot3(split(a), split(b))
+
         def second(block):
             diag = jnp.where(eye, block, 0.0)
             down = 1.0 / jnp.sum(diag, axis=1, keepdims=True)
             across = 1.0 / jnp.sum(diag, axis=0, keepdims=True)
             two = jnp.where(eye, 2.0, 0.0)
             first = down * (two - block * across)
-            return hdot(first, two - hdot(block, first))
+            return product(first, two - product(block, first))
 
         s0 = second(blk(0, 0))
         upper = blk(0, 1)
-        l10 = hdot(blk(1, 0), s0)
-        s1 = second(blk(1, 1) - hdot(l10, upper))
+        l10 = product(blk(1, 0), s0)
+        s1 = second(blk(1, 1) - product(l10, upper))
         w_ref[:B, :B] = s0
         w_ref[B:, B:] = s1
-        w_ref[:B, B:] = -hdot(s0, hdot(upper, s1))
+        w_ref[:B, B:] = -product(s0, product(upper, s1))
         w_ref[B:, :B] = jnp.zeros((B, B), F32)
         l_ref[...] = l10
 
@@ -434,9 +433,7 @@
         (um2, um134, g1, g2, g3, sg1, sg2, sg3, f1, f2, sf1, sf2, h1, sh1),
     )
     pieces = [got[k] for k in names]
-    late = marks[-2]
-    out = update_call(ids, tile, 0, late, pieces[:-1], wmat, l10, u2, None)
-    return update_call(ids, tile, late, rows, pieces[-1:], wmat, l10, u2, out)
+    return update_call(ids, tile, 0, rows, pieces, wmat, l10, u2, None)
 
 
 TAIL = 3

time: 167 us -> 173 us (1.036)
  waiting for transfers between devices: 88.2 us -> 98.5 us
  Pallas kernels: 30.1 us -> 26.5 us
    ppermute x15, waiting for transfers between devices: 60.5 us -> 70.9 us  [col_move(): return lax.ppermute(x, ('row', 'col'), pairs)]
    pallas_call x2 -> x1, Pallas kernels: 19.2 us -> 17.2 us  [update_call(): pl.pallas_call(body, out_shape=jax.ShapeDtypeStruct(tile.shape, tile.dtyp...]
  transfers between devices with their start and end apart: 36 -> 36, of which waited for: 8 -> 7; matrix products, arithmetic and copies ran while one was open for 0% -> 0% of each run, Pallas kernels for 15% -> 5%
where the time goes in v2:
time: 173 us
  waiting for transfers between devices  98.5 us (57%)
  starting transfers between devices  46.9 us (27%)
  Pallas kernels  26.5 us (15%)
    ppermute x15, waiting for transfers between devices, col_move(): return lax.ppermute(x, ('row', 'col'), pairs)  70.9 us
    ppermute x21, starting transfers between devices, row_move(): return lax.ppermute(x, 'row', pairs)  33.5 us
    ppermute x21, waiting for transfers between devices, row_move(): return lax.ppermute(x, 'row', pairs)  27.7 us
    pallas_call x1, Pallas kernels, update_call(): pl.pallas_call(body, out_shape=jax.ShapeDtypeStruct(tile.shape, tile.dtyp...  17.2 us
    ppermute x15, starting transfers between devices, col_move(): return lax.ppermute(x, ('row', 'col'), pairs)  13.4 us
    pallas_call x6, Pallas kernels, choose(): pl.pallas_call(body, out_shape=tuple((onchip(s) for s in shapes)), in_spe...  3.63 us
  transfers between devices with their start and end apart: 36, of which 7 were waited for; matrix products, arithmetic and copies ran while one was open for 0% of the time, Pallas kernels for 5%

profile of v2, /device:TPU:30, one launch (start us, length us, event | category | flops | bytes accessed | tf_op | source)
XLA Modules:
  0.0 172.7 jit_solution(14129548943753786061)
XLA Ops:
  0.0 0.1 pad_add_fusion.ids.refs_0_
  0.1 0.7 shard_map.17
  0.7 0.9 collective-permute-start.14
  1.6 0.7 collective-permute-start.13
  2.4 0.7 collective-permute-start.3
  3.1 0.7 collective-permute-start
  3.8 0.6 shard_map.21
  4.4 0.7 collective-permute-start.15
  5.1 0.7 collective-permute-start.33
  5.8 0.7 collective-permute-start.4
  6.5 0.0 collective-permute-done.33.refs_18_
  6.5 1.3 collective-permute-start.5
  7.8 0.7 collective-permute-start.1
  8.5 0.0 collective-permute-done.4.refs_1_.refs_8_
  8.6 1.3 collective-permute-start.2
  9.9 43.1 %collective-permute-done.5.refs_3_.refs_10_ = f32[256,512]{1,0:T(8,128)S(1)} collective-permute-done((f32[256,512]{1,0:T(8,128)S(1)}, f32[256,512]{1,0:T(8,128)S(1)}, u32[]{:S(2)}, u32[]{:S(2)}) %collective-permute-start.5) | collective-permute-done | bytes 524320 | tf_op jit(solution)/shard_map/ppermute | solution.py:341
  53.0 0.7 collective-permute-start.27
  53.7 0.0 collective-permute-done.1.refs_1_.refs_5_
  53.7 0.7 collective-permute-start.30
  54.4 0.6 shard_map.19.refs_1_
  55.0 0.0 collective-permute-done.15.refs_2_
  55.0 0.7 collective-permute-start.7
  55.7 1.3 collective-permute-start.21
  57.0 0.6 shard_map.22
  57.6 4.9 %collective-permute-done.2.refs_3_.refs_7_ = f32[256,512]{1,0:T(8,128)S(1)} collective-permute-done((f32[256,512]{1,0:T(8,128)S(1)}, f32[256,512]{1,0:T(8,128)S(1)}, u32[]{:S(2)}, u32[]{:S(2)}) %collective-permute-start.2) | collective-permute-done | bytes 524320 | tf_op jit(solution)/shard_map/ppermute | solution.py:341
  62.5 0.7 collective-permute-start.16
  63.2 0.6 shard_map.18.refs_0_
  63.8 0.0 collective-permute-done.27.refs_12_
  63.9 0.7 collective-permute-start.6
  64.6 0.0 collective-permute-done.30.refs_15_
  64.6 0.7 collective-permute-start.8
  65.3 0.7 collective-permute-start.9
  66.0 0.0 collective-permute-done.6.refs_2_
  66.0 1.3 collective-permute-start.11
  67.3 0.0 collective-permute-done.8.refs_4_
  67.3 1.3 collective-permute-start.10
  68.6 0.7 collective-permute-start.34
  69.3 4.5 %collective-permute-done.21.refs_8_ = f32[128,2304]{1,0:T(8,128)S(1)} collective-permute-done((f32[128,2304]{1,0:T(8,128)S(1)}, f32[128,2304]{1,0:T(8,128)S(1)}, u32[]{:S(2)}, u32[]{:S(2)}) %collective-permute-start.21) | collective-permute-done | bytes 1179680 | tf_op jit(solution)/shard_map/ppermute | solution.py:344
  73.8 13.3 %collective-permute-start.25 = (f32[128,2304]{1,0:T(8,128)S(1)}, f32[128,2304]{1,0:T(8,128)S(1)}, u32[]{:S(2)}, u32[]{:S(2)}) collective-permute-start(f32[128,2304]{1,0:T(8,128)S(1)} %collective-permute-done.21.refs_8_), channel_id=1, source_target_pairs={{24,16},{28,12},{25,17},{29,13},{26,18},{30,14},{27,19},{31,15}} | collective-permute-start | bytes 3538952 | tf_op jit(solution)/shard_map/ppermute | solution.py:344
  87.1 0.0 collective-permute-done.11.refs_7_
  87.1 0.7 collective-permute-start.18
  87.8 12.9 %collective-permute-done.10.refs_6_ = f32[256,512]{1,0:T(8,128)S(1)} collective-permute-done((f32[256,512]{1,0:T(8,128)S(1)}, f32[256,512]{1,0:T(8,128)S(1)}, u32[]{:S(2)}, u32[]{:S(2)}) %collective-permute-start.10) | collective-permute-done | bytes 524320 | tf_op jit(solution)/shard_map/ppermute | solution.py:344
  100.8 0.7 collective-permute-start.17
  101.5 1.3 collective-permute-start.22
  102.8 0.7 shard_map.20.dcore
  103.5 1.4 collective-permute-start.12
  104.9 2.2 %collective-permute-done.12.dmate = f32[512,512]{1,0:T(8,128)S(1)} collective-permute-done((f32[512,512]{1,0:T(8,128)S(1)}, f32[512,512]{1,0:T(8,128)S(1)}, u32[]{:S(2)}, u32[]{:S(2)}) %collective-permute-start.12) | collective-permute-done | bytes 1048608 | tf_op jit(solution)/shard_map/ppermute | solution.py:344
  107.1 2.3 %collective-permute-start.23 = (f32[128,2304]{1,0:T(8,128)S(1)}, f32[128,2304]{1,0:T(8,128)S(1)}, u32[]{:S(2)}, u32[]{:S(2)}) collective-permute-start(f32[128,2304]{1,0:T(8,128)S(1)} %collective-permute-done.21.refs_8_), channel_id=1, source_target_pairs={{24,28},{28,24},{25,29},{29,25},{26,30},{30,26},{27,31},{31,27}} | collective-permute-start | bytes 3538952 | tf_op jit(solution)/shard_map/ppermute | solution.py:344
  109.4 0.7 collective-permute-start.26
  110.1 0.7 collective-permute-start.19
  110.9 0.7 collective-permute-start.20
  111.6 8.0 %collective-permute-done.22.refs_9_ = f32[128,2304]{1,0:T(8,128)S(1)} collective-permute-done((f32[128,2304]{1,0:T(8,128)S(1)}, f32[128,2304]{1,0:T(8,128)S(1)}, u32[]{:S(2)}, u32[]{:S(2)}) %collective-permute-start.22) | collective-permute-done | bytes 1179680 | tf_op jit(solution)/shard_map/ppermute | solution.py:344
  119.6 1.9 %collective-permute-start.24 = (f32[128,2304]{1,0:T(8,128)S(1)}, f32[128,2304]{1,0:T(8,128)S(1)}, u32[]{:S(2)}, u32[]{:S(2)}) collective-permute-start(f32[128,2304]{1,0:T(8,128)S(1)} %collective-permute-done.22.refs_9_), channel_id=1, source_target_pairs={{24,28},{28,24},{25,29},{29,25},{26,30},{30,26},{27,31},{31,27}} | collective-permute-start | bytes 3538952 | tf_op jit(solution)/shard_map/ppermute | solution.py:344
  121.5 0.7 collective-permute-start.28
  122.2 1.3 collective-permute-start.29
  123.6 0.7 collective-permute-start.31
  124.3 1.3 collective-permute-start.32
  125.6 1.3 collective-permute-start.35
  126.9 0.0 slice-start
  126.9 3.4 %factors.1 = (f32[512,512]{1,0:T(8,128)S(1)}, f32[256,256]{1,0:T(8,128)S(1)}) custom-call(s32[2]{0:T(128)S(1)} %pad_add_fusion.ids.refs_0_, f32[512,512]{1,0:T(8,128)S(1)} %shard_map.20.dcore, f32[512,512]{1,0:T(8,128)S(1)} %collective-permute-done.12.dmate), custom_call_target="tpu_custom_call" | custom-call | tf_op jit(solution)/shard_map/factors/pallas_call | solution.py:169
  130.2 0.0 slice-start.1
  130.3 2.3 %upper_split.1.refs_4_ = bf16[1024,2304]{1,0:T(8,128)(2,1)S(1)} custom-call(s32[2]{0:T(128)S(1)} %pad_add_fusion.ids.refs_0_, f32[1152,2304]{1,0:T(8,128)} %refs_1_.1, f32[128,2304]{1,0:T(8,128)S(1)} %collective-permute-done.13.refs_1_.refs_0_, f32[384,2304]{1,0:T(8,128)S(1)} %collective-permute-done.14.refs_1_, ...), custom_call_target="tpu_custom_call" | custom-call | tf_op jit(solution)/shard_map/upper_split/pallas_call | solution.py:221
  132.6 22.8 %collective-permute-done.35.refs_19_ = f32[192,512]{1,0:T(8,128)S(1)} collective-permute-done((f32[192,512]{1,0:T(8,128)S(1)}, f32[192,512]{1,0:T(8,128)S(1)}, u32[]{:S(2)}, u32[]{:S(2)}) %collective-permute-start.35) | collective-permute-done | bytes 393248 | tf_op jit(solution)/shard_map/ppermute | solution.py:341
  155.4 17.2 %shard_map.23 = f32[1152,2304]{1,0:T(8,128)} custom-call(s32[2]{0:T(128)S(1)} %pad_add_fusion.ids.refs_0_, f32[1152,2304]{1,0:T(8,128)S(1)} %bitcast.3, f32[512,512]{1,0:T(8,128)S(1)} %get-tuple-element.18.refs_2_, f32[256,256]{1,0:T(8,128)S(1)} %get-tuple-element.19.refs_3_, bf16[1024,2304]{1,0:T(8,128)(2,1)S(1)} %upper_split.1.refs_4_, ...), custom_call_target="tpu_custom_call" | custom-call | tf_op jit(solution)/shard_map/pallas_call | solution.py:317
  (25 shorter events, 0.1 us)
Async XLA Ops:
  0.7 54.9 %collective-permute-start.14 = (f32[384,2304]{1,0:T(8,128)S(1)}, f32[384,2304]{1,0:T(8,128)S(1)}, u32[]{:S(2)}, u32[]{:S(2)}) collective-permute-start(f32[384,2304]{1,0:T(8,128)S(1)} %get-tuple-element.21), channel_id=1, source_target_pairs={{0,4},{1,5},{2,6},{3,7}} | collective-permute-start | bytes 10616840 | tf_op jit(solution)/shard_map/ppermute | solution.py:344
  1.6 2.2 %collective-permute-start.13 = (f32[128,2304]{1,0:T(8,128)S(1)}, f32[128,2304]{1,0:T(8,128)S(1)}, u32[]{:S(2)}, u32[]{:S(2)}) collective-permute-start(f32[128,2304]{1,0:T(8,128)S(1)} %get-tuple-element.20), channel_id=1, source_target_pairs={{0,4},{1,5},{2,6},{3,7}} | collective-permute-start | bytes 3538952 | tf_op jit(solution)/shard_map/ppermute | solution.py:344
  2.4 3.4 %collective-permute-start.3 = (f32[256,512]{1,0:T(8,128)S(1)}, f32[256,512]{1,0:T(8,128)S(1)}, u32[]{:S(2)}, u32[]{:S(2)}) collective-permute-start(f32[256,512]{1,0:T(8,128)S(1)} %get-tuple-element.17), channel_id=1, source_target_pairs={{0,2},{4,6},{8,10},{12,14},{16,18},{20,22},{24,26},{28,30}} | collective-permute-start | bytes 1572872 | tf_op jit(solution)/shard_map/ppermute | solution.py:341
  3.1 4.7 %collective-permute-start = (f32[256,512]{1,0:T(8,128)S(1)}, f32[256,512]{1,0:T(8,128)S(1)}, u32[]{:S(2)}, u32[]{:S(2)}) collective-permute-start(f32[256,512]{1,0:T(8,128)S(1)} %get-tuple-element.16), channel_id=1, source_target_pairs={{0,2},{4,6},{8,10},{12,14},{16,18},{20,22},{24,26},{28,30}} | collective-permute-start | bytes 1572872 | tf_op jit(solution)/shard_map/ppermute | solution.py:341
  4.4 50.6 %collective-permute-start.15 = (f32[128,2304]{1,0:T(8,128)S(1)}, f32[128,2304]{1,0:T(8,128)S(1)}, u32[]{:S(2)}, u32[]{:S(2)}) collective-permute-start(f32[128,2304]{1,0:T(8,128)S(1)} %shard_map.21), channel_id=1, source_target_pairs={{0,8},{4,20},{1,9},{5,21},{2,10},{6,22},{3,11},{7,23}} | collective-permute-start | bytes 3538952 | tf_op jit(solution)/shard_map/ppermute | solution.py:344
  5.1 1.4 collective-permute-start.33
  5.8 2.7 %collective-permute-start.4 = (f32[256,512]{1,0:T(8,128)S(1)}, f32[256,512]{1,0:T(8,128)S(1)}, u32[]{:S(2)}, u32[]{:S(2)}) collective-permute-start(f32[256,512]{1,0:T(8,128)S(1)} %collective-permute-done.3.refs_2_.refs_9_), channel_id=1, source_target_pairs={{2,1},{6,5},{10,9},{14,13},{18,17},{22,21},{26,25},{30,29}} | collective-permute-start | bytes 1572872 | tf_op jit(solution)/shard_map/ppermute | solution.py:341
  6.5 46.5 %collective-permute-start.5 = (f32[256,512]{1,0:T(8,128)S(1)}, f32[256,512]{1,0:T(8,128)S(1)}, u32[]{:S(2)}, u32[]{:S(2)}) collective-permute-start(f32[256,512]{1,0:T(8,128)S(1)} %collective-permute-done.3.refs_2_.refs_9_), channel_id=1, source_target_pairs={{2,3},{6,7},{10,11},{14,15},{18,19},{22,23},{26,27},{30,31}} | collective-permute-start | bytes 1572872 | tf_op jit(solution)/shard_map/ppermute | solution.py:341
  7.8 45.8 %collective-permute-start.1 = (f32[256,512]{1,0:T(8,128)S(1)}, f32[256,512]{1,0:T(8,128)S(1)}, u32[]{:S(2)}, u32[]{:S(2)}) collective-permute-start(f32[256,512]{1,0:T(8,128)S(1)} %collective-permute-done.refs_2_.refs_6_), channel_id=1, source_target_pairs={{2,1},{6,5},{10,9},{14,13},{18,17},{22,21},{26,25},{30,29}} | collective-permute-start | bytes 1572872 | tf_op jit(solution)/shard_map/ppermute | solution.py:341
  8.6 54.0 %collective-permute-start.2 = (f32[256,512]{1,0:T(8,128)S(1)}, f32[256,512]{1,0:T(8,128)S(1)}, u32[]{:S(2)}, u32[]{:S(2)}) collective-permute-start(f32[256,512]{1,0:T(8,128)S(1)} %collective-permute-done.refs_2_.refs_6_), channel_id=1, source_target_pairs={{2,3},{6,7},{10,11},{14,15},{18,19},{22,23},{26,27},{30,31}} | collective-permute-start | bytes 1572872 | tf_op jit(solution)/shard_map/ppermute | solution.py:341
  53.0 10.9 %collective-permute-start.27 = (f32[224,512]{1,0:T(8,128)S(1)}, f32[224,512]{1,0:T(8,128)S(1)}, u32[]{:S(2)}, u32[]{:S(2)}) collective-permute-start(f32[224,512]{1,0:T(8,128)S(1)} %get-tuple-element.24), channel_id=1, source_target_pairs={{0,2},{4,6},{8,10},{12,14},{16,18},{20,22},{24,26},{28,30}} | collective-permute-start | bytes 1376264 | tf_op jit(solution)/shard_map/ppermute | solution.py:341
  53.7 10.9 %collective-permute-start.30 = (f32[224,512]{1,0:T(8,128)S(1)}, f32[224,512]{1,0:T(8,128)S(1)}, u32[]{:S(2)}, u32[]{:S(2)}) collective-permute-start(f32[224,512]{1,0:T(8,128)S(1)} %get-tuple-element.25), channel_id=1, source_target_pairs={{0,2},{4,6},{8,10},{12,14},{16,18},{20,22},{24,26},{28,30}} | collective-permute-start | bytes 1376264 | tf_op jit(solution)/shard_map/ppermute | solution.py:341
  55.0 10.3 %collective-permute-start.7 = (f32[256,512]{1,0:T(8,128)S(1)}, f32[256,512]{1,0:T(8,128)S(1)}, u32[]{:S(2)}, u32[]{:S(2)}) collective-permute-start(f32[256,512]{1,0:T(8,128)S(1)} %shard_map.19.refs_1_), channel_id=1, source_target_pairs={{0,16},{1,17},{2,18},{3,19}} | collective-permute-start | bytes 1572872 | tf_op jit(solution)/shard_map/ppermute | solution.py:344
  55.7 18.1 %collective-permute-start.21 = (f32[128,2304]{1,0:T(8,128)S(1)}, f32[128,2304]{1,0:T(8,128)S(1)}, u32[]{:S(2)}, u32[]{:S(2)}) collective-permute-start(f32[128,2304]{1,0:T(8,128)S(1)} %collective-permute-done.15.refs_2_), channel_id=1, source_target_pairs={{8,24},{20,28},{9,25},{21,29},{10,26},{22,30},{11,27},{23,31}} | collective-permute-start | bytes 3538952 | tf_op jit(solution)/shard_map/ppermute | solution.py:344
  62.5 39.0 %collective-permute-start.16 = (f32[128,2304]{1,0:T(8,128)S(1)}, f32[128,2304]{1,0:T(8,128)S(1)}, u32[]{:S(2)}, u32[]{:S(2)}) collective-permute-start(f32[128,2304]{1,0:T(8,128)S(1)} %get-tuple-element.22), channel_id=1, source_target_pairs={{0,8},{4,20},{1,9},{5,21},{2,10},{6,22},{3,11},{7,23}} | collective-permute-start | bytes 3538952 | tf_op jit(solution)/shard_map/ppermute | solution.py:344
  63.9 2.1 %collective-permute-start.6 = (f32[256,512]{1,0:T(8,128)S(1)}, f32[256,512]{1,0:T(8,128)S(1)}, u32[]{:S(2)}, u32[]{:S(2)}) collective-permute-start(f32[256,512]{1,0:T(8,128)S(1)} %shard_map.18.refs_0_), channel_id=1, source_target_pairs={{0,8},{1,9},{2,10},{3,11}} | collective-permute-start | bytes 1572872 | tf_op jit(solution)/shard_map/ppermute | solution.py:344
  64.6 2.7 %collective-permute-start.8 = (f32[256,512]{1,0:T(8,128)S(1)}, f32[256,512]{1,0:T(8,128)S(1)}, u32[]{:S(2)}, u32[]{:S(2)}) collective-permute-start(f32[256,512]{1,0:T(8,128)S(1)} %shard_map.19.refs_1_), channel_id=1, source_target_pairs={{0,8},{1,9},{2,10},{3,11}} | collective-permute-start | bytes 1572872 | tf_op jit(solution)/shard_map/ppermute | solution.py:344
  65.3 3.3 %collective-permute-start.9 = (f32[256,512]{1,0:T(8,128)S(1)}, f32[256,512]{1,0:T(8,128)S(1)}, u32[]{:S(2)}, u32[]{:S(2)}) collective-permute-start(f32[256,512]{1,0:T(8,128)S(1)} %shard_map.18.refs_0_), channel_id=1, source_target_pairs={{0,16},{1,17},{2,18},{3,19}} | collective-permute-start | bytes 1572872 | tf_op jit(solution)/shard_map/ppermute | solution.py:344
  66.0 21.1 %collective-permute-start.11 = (f32[256,512]{1,0:T(8,128)S(1)}, f32[256,512]{1,0:T(8,128)S(1)}, u32[]{:S(2)}, u32[]{:S(2)}) collective-permute-start(f32[256,512]{1,0:T(8,128)S(1)} %collective-permute-done.7.refs_3_), channel_id=1, source_target_pairs={{16,24},{17,25},{18,26},{19,27}} | collective-permute-start | bytes 1572872 | tf_op jit(solution)/shard_map/ppermute | solution.py:344
  67.3 33.5 %collective-permute-start.10 = (f32[256,512]{1,0:T(8,128)S(1)}, f32[256,512]{1,0:T(8,128)S(1)}, u32[]{:S(2)}, u32[]{:S(2)}) collective-permute-start(f32[256,512]{1,0:T(8,128)S(1)} %collective-permute-done.6.refs_2_), channel_id=1, source_target_pairs={{8,24},{9,25},{10,26},{11,27}} | collective-permute-start | bytes 1572872 | tf_op jit(solution)/shard_map/ppermute | solution.py:344
  68.6 34.9 %collective-permute-start.34 = (f32[192,512]{1,0:T(8,128)S(1)}, f32[192,512]{1,0:T(8,128)S(1)}, u32[]{:S(2)}, u32[]{:S(2)}) collective-permute-start(f32[192,512]{1,0:T(8,128)S(1)} %collective-permute-done.33.refs_18_), channel_id=1, source_target_pairs={{2,1},{6,5},{10,9},{14,13},{18,17},{22,21},{26,25},{30,29}} | collective-permute-start | bytes 1179656 | tf_op jit(solution)/shard_map/ppermute | solution.py:341
  73.8 35.5 %collective-permute-start.25 = (f32[128,2304]{1,0:T(8,128)S(1)}, f32[128,2304]{1,0:T(8,128)S(1)}, u32[]{:S(2)}, u32[]{:S(2)}) collective-permute-start(f32[128,2304]{1,0:T(8,128)S(1)} %collective-permute-done.21.refs_8_), channel_id=1, source_target_pairs={{24,16},{28,12},{25,17},{29,13},{26,18},{30,14},{27,19},{31,15}} | collective-permute-start | bytes 3538952 | tf_op jit(solution)/shard_map/ppermute | solution.py:344
  87.1 23.0 %collective-permute-start.18 = (f32[128,2304]{1,0:T(8,128)S(1)}, f32[128,2304]{1,0:T(8,128)S(1)}, u32[]{:S(2)}, u32[]{:S(2)}) collective-permute-start(f32[128,2304]{1,0:T(8,128)S(1)} %collective-permute-done.15.refs_2_), channel_id=1, source_target_pairs={{8,12},{20,16},{9,13},{21,17},{10,14},{22,18},{11,15},{23,19}} | collective-permute-start | bytes 3538952 | tf_op jit(solution)/shard_map/ppermute | solution.py:344
  100.8 10.1 %collective-permute-start.17 = (f32[128,2304]{1,0:T(8,128)S(1)}, f32[128,2304]{1,0:T(8,128)S(1)}, u32[]{:S(2)}, u32[]{:S(2)}) collective-permute-start(f32[128,2304]{1,0:T(8,128)S(1)} %get-tuple-element.23), channel_id=1, source_target_pairs={{0,8},{4,20},{1,9},{5,21},{2,10},{6,22},{3,11},{7,23}} | collective-permute-start | bytes 3538952 | tf_op jit(solution)/shard_map/ppermute | solution.py:344
  101.5 18.1 %collective-permute-start.22 = (f32[128,2304]{1,0:T(8,128)S(1)}, f32[128,2304]{1,0:T(8,128)S(1)}, u32[]{:S(2)}, u32[]{:S(2)}) collective-permute-start(f32[128,2304]{1,0:T(8,128)S(1)} %collective-permute-done.16.refs_3_), channel_id=1, source_target_pairs={{8,24},{20,28},{9,25},{21,29},{10,26},{22,30},{11,27},{23,31}} | collective-permute-start | bytes 3538952 | tf_op jit(solution)/shard_map/ppermute | solution.py:344
  103.5 3.6 %collective-permute-start.12 = (f32[512,512]{1,0:T(8,128)S(1)}, f32[512,512]{1,0:T(8,128)S(1)}, u32[]{:S(2)}, u32[]{:S(2)}) collective-permute-start(f32[512,512]{1,0:T(8,128)S(1)} %shard_map.20.dcore), channel_id=1, source_target_pairs={{0,4},{8,12},{16,20},{24,28},{1,5},{9,13},{17,21},{25,29},{2,6},{1... | collective-permute-start | bytes 3145736 | tf_op jit(solution)/shard_map/ppermute | solution.py:344
  107.1 14.5 %collective-permute-start.23 = (f32[128,2304]{1,0:T(8,128)S(1)}, f32[128,2304]{1,0:T(8,128)S(1)}, u32[]{:S(2)}, u32[]{:S(2)}) collective-permute-start(f32[128,2304]{1,0:T(8,128)S(1)} %collective-permute-done.21.refs_8_), channel_id=1, source_target_pairs={{24,28},{28,24},{25,29},{29,25},{26,30},{30,26},{27,31},{31,27}} | collective-permute-start | bytes 3538952 | tf_op jit(solution)/shard_map/ppermute | solution.py:344
  109.4 12.9 %collective-permute-start.26 = (f32[128,2304]{1,0:T(8,128)S(1)}, f32[128,2304]{1,0:T(8,128)S(1)}, u32[]{:S(2)}, u32[]{:S(2)}) collective-permute-start(f32[128,2304]{1,0:T(8,128)S(1)} %collective-permute-done.25.refs_12_), channel_id=1, source_target_pairs={{12,8},{16,20},{13,9},{17,21},{14,10},{18,22},{15,11},{19,23}} | collective-permute-start | bytes 3538952 | tf_op jit(solution)/shard_map/ppermute | solution.py:344
  110.1 13.4 %collective-permute-start.19 = (f32[128,2304]{1,0:T(8,128)S(1)}, f32[128,2304]{1,0:T(8,128)S(1)}, u32[]{:S(2)}, u32[]{:S(2)}) collective-permute-start(f32[128,2304]{1,0:T(8,128)S(1)} %collective-permute-done.16.refs_3_), channel_id=1, source_target_pairs={{8,12},{20,16},{9,13},{21,17},{10,14},{22,18},{11,15},{23,19}} | collective-permute-start | bytes 3538952 | tf_op jit(solution)/shard_map/ppermute | solution.py:344
  110.9 13.4 %collective-permute-start.20 = (f32[128,2304]{1,0:T(8,128)S(1)}, f32[128,2304]{1,0:T(8,128)S(1)}, u32[]{:S(2)}, u32[]{:S(2)}) collective-permute-start(f32[128,2304]{1,0:T(8,128)S(1)} %collective-permute-done.17.refs_4_), channel_id=1, source_target_pairs={{8,12},{20,16},{9,13},{21,17},{10,14},{22,18},{11,15},{23,19}} | collective-permute-start | bytes 3538952 | tf_op jit(solution)/shard_map/ppermute | solution.py:344
  119.6 6.0 %collective-permute-start.24 = (f32[128,2304]{1,0:T(8,128)S(1)}, f32[128,2304]{1,0:T(8,128)S(1)}, u32[]{:S(2)}, u32[]{:S(2)}) collective-permute-start(f32[128,2304]{1,0:T(8,128)S(1)} %collective-permute-done.22.refs_9_), channel_id=1, source_target_pairs={{24,28},{28,24},{25,29},{29,25},{26,30},{30,26},{27,31},{31,27}} | collective-permute-start | bytes 3538952 | tf_op jit(solution)/shard_map/ppermute | solution.py:344
  121.5 33.8 %collective-permute-start.28 = (f32[224,512]{1,0:T(8,128)S(1)}, f32[224,512]{1,0:T(8,128)S(1)}, u32[]{:S(2)}, u32[]{:S(2)}) collective-permute-start(f32[224,512]{1,0:T(8,128)S(1)} %collective-permute-done.27.refs_12_), channel_id=1, source_target_pairs={{2,1},{6,5},{10,9},{14,13},{18,17},{22,21},{26,25},{30,29}} | collective-permute-start | bytes 1376264 | tf_op jit(solution)/shard_map/ppermute | solution.py:341
  122.2 33.1 %collective-permute-start.29 = (f32[224,512]{1,0:T(8,128)S(1)}, f32[224,512]{1,0:T(8,128)S(1)}, u32[]{:S(2)}, u32[]{:S(2)}) collective-permute-start(f32[224,512]{1,0:T(8,128)S(1)} %collective-permute-done.27.refs_12_), channel_id=1, source_target_pairs={{2,3},{6,7},{10,11},{14,15},{18,19},{22,23},{26,27},{30,31}} | collective-permute-start | bytes 1376264 | tf_op jit(solution)/shard_map/ppermute | solution.py:341
  123.6 31.8 %collective-permute-start.31 = (f32[224,512]{1,0:T(8,128)S(1)}, f32[224,512]{1,0:T(8,128)S(1)}, u32[]{:S(2)}, u32[]{:S(2)}) collective-permute-start(f32[224,512]{1,0:T(8,128)S(1)} %collective-permute-done.30.refs_15_), channel_id=1, source_target_pairs={{2,1},{6,5},{10,9},{14,13},{18,17},{22,21},{26,25},{30,29}} | collective-permute-start | bytes 1376264 | tf_op jit(solution)/shard_map/ppermute | solution.py:341
  124.3 31.1 %collective-permute-start.32 = (f32[224,512]{1,0:T(8,128)S(1)}, f32[224,512]{1,0:T(8,128)S(1)}, u32[]{:S(2)}, u32[]{:S(2)}) collective-permute-start(f32[224,512]{1,0:T(8,128)S(1)} %collective-permute-done.30.refs_15_), channel_id=1, source_target_pairs={{2,3},{6,7},{10,11},{14,15},{18,19},{22,23},{26,27},{30,31}} | collective-permute-start | bytes 1376264 | tf_op jit(solution)/shard_map/ppermute | solution.py:341
  125.6 29.7 %collective-permute-start.35 = (f32[192,512]{1,0:T(8,128)S(1)}, f32[192,512]{1,0:T(8,128)S(1)}, u32[]{:S(2)}, u32[]{:S(2)}) collective-permute-start(f32[192,512]{1,0:T(8,128)S(1)} %collective-permute-done.33.refs_18_), channel_id=1, source_target_pairs={{2,3},{6,7},{10,11},{14,15},{18,19},{22,23},{26,27},{30,31}} | collective-permute-start | bytes 1179656 | tf_op jit(solution)/shard_map/ppermute | solution.py:341
  126.9 28.5 %slice-start = ((s8[10616832]{0:T(1024)(128)(4,1)}), s8[4194304]{0:T(1024)(128)(4,1)S(1)}, s32[]{:S(2)}) async-start(s8[10616832]{0:T(1024)(128)(4,1)} %bitcast.2), calls=%async_computation | async-start | bytes 8388608
  130.2 25.1 %slice-start.1 = ((s8[10616832]{0:T(1024)(128)(4,1)}), s8[4194304]{0:T(1024)(128)(4,1)S(1)}, s32[]{:S(2)}) async-start(s8[10616832]{0:T(1024)(128)(4,1)} %bitcast.2), calls=%async_computation.1 | async-start | bytes 8388608
  130.3 25.1 %slice-start.2 = ((s8[10616832]{0:T(1024)(128)(4,1)}), s8[2228224]{0:T(1024)(128)(4,1)S(1)}, s32[]{:S(2)}) async-start(s8[10616832]{0:T(1024)(128)(4,1)} %bitcast.2), calls=%async_computation.2 | async-start | bytes 4456448
